TPU v7x, 32 devices: a whole 2x2x4 slice. The times are simulated.
32 devices in a mesh: pts: 4 (over y, core), ctr: 8 (over z, x).
Axes of the slice: x: 2, y: 2, z: 4, core: 2. Of those that a mesh axis runs over, the one named last changes fastest.
Arguments:
- points: bfloat16 [512, 512], P(('pts', 'ctr')), may hold values from -6 to 6
- point_class: int32 [512], P(('pts', 'ctr')), may hold values from 0 to 7
- targets: float32 [512, 128], P(('pts', 'ctr')), may hold values from -6 to 6
- class_weight: float32 [8], replicated, may hold values from 0.25 to 4
- inv_scale: float32 [512], replicated, may hold values from 0.003 to 0.3
- centers: bfloat16 [32768, 512], P('ctr'), may hold values from -6 to 6
- coefficients: bfloat16 [32768, 128], P('ctr'), may hold values from -2.5 to 2.5
- center_index: int32 [4096], replicated, may hold values from 0 to 32767, as said below
- factor: float32 [4096, 4096], P('ctr'), as said below
- panel_inverse: float32 [4096, 2048], P('ctr'), as said below
Outputs:
- gradient: float32 [32768, 128], P('ctr', 'pts')
- solved: float32 [4096, 128], P('ctr', 'pts')
Inputs may be any that keep to these rules, and one draw needn't show every extreme that they name: `center_index`: the values are distinct; window row r lies in the center shard (index of ctr, 4096 centers each) numbered order[r mod 8] for one permutation order of the shards, so each shard holds exactly 512 window rows and the 512 rows of each aligned block of the window hold at most 64 of one shard's centers, a bound that is reached. factor is lower triangular with its diagonal between 1 and 2. `panel_inverse`: the rows of panel p hold the inverse of factor's diagonal block of rows and columns p * 2048 to (p + 1) * 2048 - 1.
All inputs are finite; a program needn't handle non-finite values.
Results may differ from a plain program's by a relative error of at most 0.0055.
Values may be sent and summed in bfloat16 or wider, within the bound.
A program may use at most 64 MiB of HBM per device.

v0:
```python
import jax
import jax.numpy as jnp
from jax import lax
from jax.sharding import PartitionSpec as P


def gaussian(samples, anchors):
    products = lax.dot_general(
        samples, anchors, (((1,), (1,)), ((), ())), preferred_element_type=jnp.float32
    )
    left_norm = jnp.sum(jnp.square(samples.astype(jnp.float32)), axis=1)
    right_norm = jnp.sum(jnp.square(anchors.astype(jnp.float32)), axis=1)
    exponent = products - 0.5 * left_norm[:, None] - 0.5 * right_norm[None, :]
    return jnp.exp(exponent).astype(jnp.bfloat16)


def class_lookup(labels, table):
    classes = jnp.arange(table.shape[0], dtype=jnp.int32)
    return jnp.sum(jnp.where(labels[:, None] == classes[None, :], table[None, :], 0.0), axis=1)


def window_slots(center_index, shard_rows, blocks):
    owner = (center_index // shard_rows).reshape(blocks, -1)
    block_len = owner.shape[1]
    position = jnp.arange(block_len, dtype=jnp.int32)
    earlier = (owner[:, :, None] == owner[:, None, :]) & (
        position[None, None, :] < position[None, :, None]
    )
    return (owner, jnp.sum(earlier.astype(jnp.int32), axis=2))


def body(
    points,
    point_class,
    targets,
    class_weight,
    inv_scale,
    centers,
    coefficients,
    center_index,
    factor,
    panel_inverse,
):
    own_scaled = (points.astype(jnp.float32) * inv_scale[None, :]).astype(jnp.bfloat16)
    group_rows = lax.all_gather(own_scaled, "ctr", axis=0, tiled=True)
    scaled_centers = (centers.astype(jnp.float32) * inv_scale[None, :]).astype(jnp.bfloat16)
    kernel = gaussian(group_rows, scaled_centers)
    partial_value = jnp.dot(kernel, coefficients, preferred_element_type=jnp.float32)
    own_weight = class_lookup(point_class, class_weight)
    summed = lax.psum(partial_value, "ctr")
    group_targets, group_weight = (
        lax.all_gather(targets, "ctr", axis=0, tiled=True),
        lax.all_gather(own_weight, "ctr", axis=0, tiled=True),
    )
    residual = (group_weight[:, None] * (summed - group_targets)).astype(jnp.bfloat16)
    backward = lax.dot_general(
        kernel, residual, (((0,), (0,)), ((), ())), preferred_element_type=jnp.float32
    )
    gradient = lax.psum_scatter(backward, "pts", scatter_dimension=1, tiled=True)
    row_count = gradient.shape[0]
    shard_index = lax.axis_index("ctr")
    relative = center_index - shard_index * row_count
    inside = (relative >= 0) & (relative < row_count)
    picked = jnp.take(gradient, jnp.clip(relative, 0, row_count - 1), axis=0)
    blocks = lax.axis_size("ctr")
    block_len = center_index.shape[0] // blocks
    slot_cap = (block_len + blocks - 1) // blocks
    owner, slot = window_slots(center_index, row_count, blocks)
    block_of = jnp.arange(blocks, dtype=jnp.int32)[:, None]
    target_slot = jnp.where(
        inside.reshape(blocks, block_len), block_of * slot_cap + slot, blocks * slot_cap
    )
    outgoing = jnp.zeros((blocks * slot_cap, picked.shape[1]), jnp.float32)
    outgoing = outgoing.at[target_slot.reshape(-1)].set(picked, mode="drop")
    incoming = lax.all_to_all(outgoing, "ctr", split_axis=0, concat_axis=0, tiled=True)
    own_owner = lax.dynamic_index_in_dim(owner, shard_index, 0, keepdims=False)
    own_slot = lax.dynamic_index_in_dim(slot, shard_index, 0, keepdims=False)
    rhs_own = jnp.take(incoming, own_owner * slot_cap + own_slot, axis=0)
    own_rows = rhs_own.shape[0]
    panel_rows = panel_inverse.shape[1]
    panel_count = factor.shape[1] // panel_rows
    own_panel = shard_index * own_rows // panel_rows
    solved_full = jnp.zeros((factor.shape[1], rhs_own.shape[1]), jnp.float32)
    solved = jnp.zeros_like(rhs_own)
    for current in range(panel_count):
        reduced = rhs_own
        if current > 0:
            reduced = rhs_own - jnp.dot(factor, solved_full, precision=lax.Precision.HIGHEST)
        gathered = lax.all_gather(reduced, "ctr", axis=0, tiled=True)
        begin = current * panel_rows
        panel_part = jnp.dot(
            panel_inverse, gathered[begin : begin + panel_rows], precision=lax.Precision.HIGHEST
        )
        panel_part = jnp.where(own_panel == current, panel_part, 0.0)
        solved = solved + panel_part
        if current + 1 < panel_count:
            solved_full = lax.all_gather(panel_part, "ctr", axis=0, tiled=True)
    return (gradient, solved)


def solution(mesh):
    placed = (
        P(("pts", "ctr"), None),
        P(("pts", "ctr")),
        P(("pts", "ctr"), None),
        P(),
        P(),
        P("ctr", None),
        P("ctr", None),
        P(),
        P("ctr", None),
        P("ctr", None),
    )
    return jax.shard_map(
        body,
        mesh=mesh,
        in_specs=placed,
        out_specs=(P("ctr", "pts"), P("ctr", "pts")),
        check_vma=False,
    )
```

profile of v0, /device:TPU:0, one launch (start us, length us, event | category | flops | bytes accessed | tf_op | source)
XLA Modules:
  0.0 314.4 jit_solution(2754512657936693553)
XLA Ops:
  7.2 0.9 multiply_convert_fusion.4
  8.1 32.5 %all_gather.18 = bf16[128,512]{1,0:T(8,128)(2,1)S(1)} all-gather(bf16[16,512]{1,0:T(8,128)(2,1)S(1)} %multiply_convert_fusion.4), channel_id=1, replica_groups=mesh['pts'=4,'ctr'=8] {'ctr'}, dimensions={0}, use_global_device_ids=true | all-gather | bytes 147456 | tf_op jit(solution)/shard_map/all_gather | solution.py:45
  40.6 3.4 %multiply_reduce_fusion = f32[4096]{0:T(1024)S(1)} fusion(f32[512]{0:T(512)} %param.14, bf16[4096,512]{1,0:T(8,128)(2,1)} %param.15), kind=kLoop, calls=%fused_computation.4 | loop fusion | flops 12578816 | bytes 4212736 | tf_op jit(solution)/shard_map/reduce_sum | solution.py:12
  44.2 1.6 fusion.2
  45.8 1.1 fusion.20
  48.5 21.3 %all-reduce = f32[128]{0:T(128)S(1)} all-reduce(f32[128]{0:T(128)S(1)} %dynamic-update-slice), channel_id=1, replica_groups=mesh['pts'=4,'ctr'=8] {'ctr'}, use_global_device_ids=true, to_apply=%add | all-reduce | flops 128 | bytes 1024
  69.8 30.5 %all_gather.20 = f32[128,128]{1,0:T(8,128)S(1)} all-gather(f32[16,128]{1,0:T(8,128)S(1)} %copy-done.5), channel_id=1, replica_groups=mesh['pts'=4,'ctr'=8] {'ctr'}, dimensions={0}, use_global_device_ids=true | all-gather | bytes 73728 | tf_op jit(solution)/shard_map/all_gather | solution.py:52
  100.3 16.9 %all-reduce.3.cloned.1.call-done = f32[128,128]{1,0:T(8,128)} async-done(((f32[128,128]{1,0:T(8,128)}), f32[128,128]{1,0:T(8,128)}) %all-reduce.3.cloned.1.call-update) | async-done | bytes 65552 | tf_op jit(solution)/shard_map/psum | solution.py:50
  117.2 2.7 fusion.14
  120.1 2.2 convert_reduce_fusion
  122.5 28.9 %reduce-scatter.2.cloned.1.call-done = f32[4096,32]{0,1:T(8,128)} async-done(((f32[4096,128]{0,1:T(8,128)}), f32[4096,32]{0,1:T(8,128)}) %reduce-scatter.2.cloned.1.call-update) | async-done | bytes 524304 | tf_op jit(solution)/shard_map/reduce_scatter | solution.py:59
  151.4 1.6 copy.26
  153.0 23.7 %scatter_custom_fusion = f32[512,32]{1,0:T(8,128)S(1)} fusion(s32[4096]{0:T(1024)S(1)} %get-tuple-element.5, f32[]{:T(128)} %constant.83.clone.1, pred[4096]{0:T(1024)(128)(4,1)S(1)} %compare_and_fusion, f32[]{:T(128)} %constant.49.clone.1, f32[4096,32]{1,0:T(8,128)S(1)} %copy.26, s32[4096]{0:T(1024)S(1)} %get-tuple-element.4), kind=kCustom, calls=%fused_computation.10 | custom fusion | flops 131072 | bytes 2183176 | tf_op jit(solution)/shard_map/scatter | solution.py:74
  176.8 0.8 reshape.138
  177.6 5.5 %all-to-all-start = ((f32[8,1,2048]{2,1,0:T(1,128)}), f32[8,1,2048]{2,1,0:T(1,128)S(1)}, u32[]{:S(2)}, u32[]{:S(2)}) async-start(f32[8,1,2048]{2,1,0:T(1,128)} %reshape.138), calls=%async_computation.1 | async-start | bytes 131072 | tf_op jit(solution)/shard_map/all_to_all | solution.py:75
  183.2 6.9 %all-to-all-done = f32[8,1,2048]{2,1,0:T(1,128)S(1)} async-done(((f32[8,1,2048]{2,1,0:T(1,128)}), f32[8,1,2048]{2,1,0:T(1,128)S(1)}, u32[]{:S(2)}, u32[]{:S(2)}) %all-to-all-start) | async-done | bytes 65568 | tf_op jit(solution)/shard_map/all_to_all | solution.py:75
  190.6 0.8 reduce
  191.6 1.0 gather_fusion
  192.7 31.6 %all_gather.21 = f32[4096,32]{0,1:T(8,128)S(1)} all-gather(f32[512,32]{0,1:T(8,128)S(1)} %broadcast_select_fusion), channel_id=1, replica_groups=mesh['pts'=4,'ctr'=8] {'ctr'}, dimensions={0}, use_global_device_ids=true | all-gather | bytes 589824 | tf_op jit(solution)/shard_map/all_gather | solution.py:89
  224.4 6.0 %fusion.7 = f32[512,32]{0,1:T(8,128)S(1)} fusion(f32[512,2048]{1,0:T(8,128)} %param.19, f32[4096,32]{0,1:T(8,128)S(1)} %all_gather.21, pred[]{:T(512)S(6)} %eq.35), kind=kOutput, calls=%fused_computation.17 | convolution fusion | flops 402669568 | bytes 4521985 | tf_op jit(solution)/shard_map/dot_general | solution.py:91
  230.4 31.5 %all_gather.22 = f32[4096,32]{0,1:T(8,128)S(1)} all-gather(f32[512,32]{0,1:T(8,128)S(1)} %fusion.7), channel_id=1, replica_groups=mesh['pts'=4,'ctr'=8] {'ctr'}, dimensions={0}, use_global_device_ids=true | all-gather | bytes 589824 | tf_op jit(solution)/shard_map/all_gather | solution.py:97
  261.9 9.9 %fusion.5 = f32[512,32]{0,1:T(8,128)S(1)} fusion(f32[512,32]{0,1:T(8,128)S(1)} %broadcast_select_fusion, f32[4096,32]{0,1:T(8,128)S(1)} %all_gather.22, f32[512,4096]{1,0:T(8,128)} %param.18), kind=kOutput, calls=%fused_computation.13 | convolution fusion | flops 805322752 | bytes 9043968 | tf_op jit(solution)/shard_map/dot_general | solution.py:88
  271.8 31.2 %all_gather.23 = f32[4096,32]{0,1:T(8,128)S(1)} all-gather(f32[512,32]{0,1:T(8,128)S(1)} %fusion.5), channel_id=1, replica_groups=mesh['pts'=4,'ctr'=8] {'ctr'}, dimensions={0}, use_global_device_ids=true | all-gather | bytes 589824 | tf_op jit(solution)/shard_map/all_gather | solution.py:89
  303.0 4.5 %fusion.8 = f32[512,32]{0,1:T(8,128)} fusion(f32[512,32]{0,1:T(8,128)S(1)} %fusion.7, f32[512,2048]{1,0:T(8,128)S(1)} %copy-done.1, f32[4096,32]{0,1:T(8,128)S(1)} %all_gather.23, pred[]{:T(512)S(6)} %eq.39), kind=kOutput, calls=%fused_computation.18 | convolution fusion | flops 402685952 | bytes 4587521 | tf_op jit(solution)/shard_map/dot_general | solution.py:91
  (46 shorter events, 2.4 us)
Async XLA Ops:
  7.2 38.6 %copy-start = (bf16[4096,128]{1,0:T(8,128)(2,1)S(1)}, bf16[4096,128]{1,0:T(8,128)(2,1)}, u32[]{:S(2)}) copy-start(bf16[4096,128]{1,0:T(8,128)(2,1)} %param.16) | copy-start | bytes 3145732
  7.2 36.9 %copy-start.4 = (f32[512]{0:T(512)S(1)}, f32[512]{0:T(512)}, u32[]{:S(2)}) copy-start(f32[512]{0:T(512)} %param.14) | copy-start | bytes 6148
  7.2 110.0 %all-reduce.3.cloned.1.call-start = ((), (), s32[]{:S(2)}) async-start(), calls=%async_computation.2 | async-start | bytes 131072 | tf_op jit(solution)/shard_map/psum | solution.py:50
  7.2 36.9 %copy-start.2 = (bf16[4096,512]{1,0:T(8,128)(2,1)S(1)}, bf16[4096,512]{1,0:T(8,128)(2,1)}, u32[]{:S(2)}) copy-start(bf16[4096,512]{1,0:T(8,128)(2,1)} %param.15) | copy-start | bytes 12582916
  44.1 2.8 copy-start.6
  44.1 2.8 copy-start.7
  44.1 2.9 copy-start.8
  44.1 25.6 %copy-start.5 = (f32[16,128]{1,0:T(8,128)S(1)}, f32[16,128]{1,0:T(8,128)}, u32[]{:S(2)}) copy-start(f32[16,128]{1,0:T(8,128)} %param.12) | copy-start | bytes 24580
  45.7 74.2 %copy-start.3 = (s32[4096]{0:T(1024)S(1)}, s32[4096]{0:T(1024)}, u32[]{:S(2)}) copy-start(s32[4096]{0:T(1024)} %param.17) | copy-start | bytes 49156
  46.8 104.6 %reduce-scatter.2.cloned.1.call-start = ((), (), s32[]{:S(2)}) async-start(), calls=%async_computation.3 | async-start | bytes 2621440 | tf_op jit(solution)/shard_map/reduce_scatter | solution.py:59
  177.6 12.4 %all-to-all-start = ((f32[8,1,2048]{2,1,0:T(1,128)}), f32[8,1,2048]{2,1,0:T(1,128)S(1)}, u32[]{:S(2)}, u32[]{:S(2)}) async-start(f32[8,1,2048]{2,1,0:T(1,128)} %reshape.138), calls=%async_computation.1 | async-start | bytes 131072 | tf_op jit(solution)/shard_map/all_to_all | solution.py:75
  261.9 41.1 %copy-start.1 = (f32[512,2048]{1,0:T(8,128)S(1)}, f32[512,2048]{1,0:T(8,128)}, u32[]{:S(2)}) copy-start(f32[512,2048]{1,0:T(8,128)} %param.19) | copy-start | bytes 12582916
Sparse Core Ops, SparseCore 0:
  47.0 70.1 all-reduce.2
  120.3 31.0 reduce-scatter.1
where the time goes:
time: 315 us; the launch traced here: 314 us
  blocking collectives  179 us (57%)
  waiting for transfers between devices  52.7 us (17%)
  other arithmetic  31.4 us (10%)
  matrix products  25.8 us (8%)
  between operations  15 us (5%)
  starting transfers between devices  5.6 us (2%)
  local copies, waits for them, and re-layouts  5.28 us (2%)
    all_gather x2, blocking collectives, body(): gathered = lax.all_gather(reduced, 'ctr', axis=0, tiled=True)  62.8 us
    all_gather x1, blocking collectives, body(): group_rows = lax.all_gather(own_scaled, 'ctr', axis=0, tiled=True)  32.5 us
    all_gather x1, blocking collectives, body(): solved_full = lax.all_gather(panel_part, 'ctr', axis=0, tiled=True)  31.5 us
    all_gather x1, blocking collectives, body(): lax.all_gather(targets, 'ctr', axis=0, tiled=True)  30.5 us
    reduce_scatter x1, waiting for transfers between devices, body(): lax.psum_scatter(backward, 'pts', scatter_dimension=1, tiled=True)  28.9 us
    scatter x1, other arithmetic, body(): outgoing = outgoing.at[target_slot.reshape(-1)].set(picked, mode='drop')  23.7 us
    unnamed x1, blocking collectives  21.3 us
    psum x1, waiting for transfers between devices, body(): summed = lax.psum(partial_value, 'ctr')  16.9 us
  transfers between devices with their start and end apart: 3, of which 3 were waited for; matrix products, arithmetic and copies ran while one was open for 1% of the time, Pallas kernels for 0%

commit v1 on v0

v1 whole, which is shorter than its diff:
```python
import functools

import jax
import jax.numpy as jnp
from jax import lax
from jax.experimental import pallas as pl
from jax.experimental.pallas import tpu as pltpu
from jax.sharding import PartitionSpec as P

MESH = pl.DeviceIdType.MESH
NT = (((1,), (1,)), ((), ()))
F32 = jnp.float32
BF16 = jnp.bfloat16


def dot_nt(left, right):
    return lax.dot_general(left, right, NT, preferred_element_type=F32)


def kernel(
    n_pts, n_ctr, panels, chunk,
    order_ref, pts_ref, cls_ref, tgt_ref, cw_ref, inv_ref, sel_ref, cen_hbm, coef_hbm, fac_hbm, pinv_hbm,
    grad_ref, sol_ref,
    cen, coef, pinv_raw, pinv, fac_raw, fac, rnorm, pall, kmat, ksel,
    part, part_recv, rall, wsend, wrecv, wpack, wblk, solsend, solrecv, rhssend, rhsrecv,
    loc, pt_s, pt_r, fw_s, fw_r, pr_s, pr_r, rs_s, rs_r, w_s, w_r, so_s, so_r, rh_s, rh_r,
):
    p_me, c_me = lax.axis_index("pts"), lax.axis_index("ctr")
    rows = pts_ref.shape[0]
    group = rows * n_ctr
    centers = cen.shape[0]
    feats = cen.shape[1]
    targets = tgt_ref.shape[1]
    tcols = targets // n_pts
    own_rows = pinv.shape[0]
    panel_rows = pinv.shape[1]
    owners = panel_rows // own_rows
    my_panel = c_me // owners
    chunks = centers // chunk

    def remote(src, dst, send, recv, p, c):
        return pltpu.make_async_remote_copy(
            src_ref=src, dst_ref=dst, send_sem=send, recv_sem=recv,
            device_id={"pts": p, "ctr": c}, device_id_type=MESH,
        )

    def each(n, fn):
        def step(k, carry):
            fn(k)
            return carry
        lax.fori_loop(0, n, step, 0)

    barrier = pltpu.get_barrier_semaphore()
    everyone = n_pts * n_ctr
    me = p_me * n_ctr + c_me

    def greet(k):
        other = lax.rem(me + k + 1, everyone)
        pl.semaphore_signal(
            barrier, inc=1,
            device_id={"pts": other // n_ctr, "ctr": lax.rem(other, n_ctr)}, device_id_type=MESH,
        )
    each(everyone - 1, greet)

    cen_copy = pltpu.make_async_copy(cen_hbm, cen, loc.at[0])
    coef_copy = pltpu.make_async_copy(coef_hbm, coef, loc.at[1])
    pinv_copy = pltpu.make_async_copy(pinv_hbm, pinv_raw, loc.at[2])
    fac_copy = pltpu.make_async_copy(fac_hbm.at[:, pl.ds(0, fac.shape[1])], fac_raw, loc.at[3])
    for copy in (cen_copy, coef_copy, pinv_copy, fac_copy):
        copy.start()

    inv = inv_ref[...]
    own_slot = pl.ds(pl.multiple_of(me * rows, rows), rows)
    pall[own_slot, :] = (pts_ref[...].astype(F32) * inv).astype(BF16)
    pl.semaphore_wait(barrier, everyone - 1)

    def pt_copy(c_src, c_dst):
        slot = pl.ds(pl.multiple_of((p_me * n_ctr + c_src) * rows, rows), rows)
        return remote(pall.at[slot], pall.at[slot], pt_s.at[c_dst], pt_r.at[c_src], p_me, c_dst)

    def peer(k):
        return lax.rem(c_me + k + 1, n_ctr)
    each(n_ctr - 1, lambda k: pt_copy(c_me, peer(k)).start())

    ones = jnp.ones((8, feats), BF16)
    cen_copy.wait()

    def scale(k):
        at = pl.ds(pl.multiple_of(k * chunk, chunk), chunk)
        scaled = (cen[at, :].astype(F32) * inv).astype(BF16)
        cen[at, :] = scaled
        square = jnp.square(scaled.astype(F32))
        high = square.astype(BF16)
        low = (square - high.astype(F32)).astype(BF16)
        rnorm[:, at] = 0.5 * (dot_nt(ones, high) + dot_nt(ones, low))
    each(chunks, scale)
    coef_copy.wait()

    each(n_ctr - 1, lambda k: pt_copy(peer(k), peer(k)).wait_recv())

    def group_at(p):
        return pl.ds(pl.multiple_of(p * group, group), group)

    def fw_copy(p_src, p_dst):
        at = group_at(p_src)
        return remote(pall.at[at], pall.at[at], fw_s.at[p_dst], fw_r.at[p_src], p_dst, c_me)

    def mate(k):
        return lax.rem(p_me + k + 1, n_pts)
    each(n_pts - 1, lambda k: fw_copy(p_me, mate(k)).start())

    def half_norm(x):
        return 0.5 * jnp.sum(jnp.square(x.astype(F32)), axis=1, keepdims=True)

    def kernel_block(p, k):
        at = pl.ds(pl.multiple_of(k * chunk, chunk), chunk)
        mine = pall[group_at(p), :]
        exponent = dot_nt(mine, cen[at, :]) - half_norm(mine) - rnorm[0:1, at]
        block = jnp.exp(exponent).astype(BF16)
        kmat[group_at(p), at] = block
        return block, at

    def forward(k, total):
        block, at = kernel_block(p_me, k)
        return total + jnp.dot(block, coef[at, :], preferred_element_type=F32)
    total = lax.fori_loop(0, chunks, forward, jnp.zeros((group, targets), F32))
    part[...] = total.reshape(n_ctr, rows, targets)

    def pr_copy(c_src, c_dst):
        return remote(part.at[c_dst], part_recv.at[c_src], pr_s.at[c_dst], pr_r.at[c_src], p_me, c_dst)
    each(n_ctr - 1, lambda k: pr_copy(c_me, peer(k)).start())

    pinv_copy.wait()
    pinv[...] = pinv_raw[...].astype(BF16)
    fac_copy.wait()
    fac[...] = fac_raw[...].astype(BF16)

    each(n_ctr - 1, lambda k: pr_copy(peer(k), peer(k)).wait_recv())
    part_recv[c_me] = part[c_me]
    predicted = jnp.sum(part_recv[...], axis=0)
    classes = lax.broadcasted_iota(jnp.int32, (rows, cw_ref.shape[1]), 1)
    weight = jnp.sum(jnp.where(cls_ref[...] == classes, cw_ref[...], 0.0), axis=1, keepdims=True)
    rall[own_slot, :] = (weight * (predicted - tgt_ref[...])).astype(BF16)

    def rs_copy(src, dst):
        slot = pl.ds(pl.multiple_of(src * rows, rows), rows)
        return remote(
            rall.at[slot], rall.at[slot], rs_s.at[dst], rs_r.at[src], dst // n_ctr, lax.rem(dst, n_ctr)
        )

    def other(k):
        return lax.rem(me + k + 1, everyone)
    each(everyone - 1, lambda k: rs_copy(me, other(k)).start())

    each(n_pts - 1, lambda k: fw_copy(mate(k), mate(k)).wait_recv())

    def rest(k):
        kernel_block(mate(k // chunks), lax.rem(k, chunks))
    each((n_pts - 1) * chunks, rest)

    chosen = (sel_ref[...].astype(F32) * inv).astype(BF16)
    chosen_norm = half_norm(chosen)

    def window_kernel(p):
        mine = pall[group_at(p), :]
        square = jnp.square(mine.astype(F32))
        high = square.astype(BF16)
        low = (square - high.astype(F32)).astype(BF16)
        norm = 0.5 * (dot_nt(ones, high) + dot_nt(ones, low))
        ksel[:, group_at(p)] = jnp.exp(dot_nt(chosen, mine) - norm[0:1] - chosen_norm).astype(BF16)
    each(n_pts, window_kernel)

    each(everyone - 1, lambda k: rs_copy(other(k), other(k)).wait_recv())

    source = lax.broadcasted_iota(jnp.int32, (targets, targets), 0)
    lane = lax.broadcasted_iota(jnp.int32, (targets, targets), 1)
    pick = (source == p_me * tcols + lax.rem(lane, tcols)).astype(BF16)
    wide = jnp.dot(rall[...], pick, preferred_element_type=F32).astype(BF16)
    window = jnp.dot(ksel[...], wide, preferred_element_type=F32)
    run = wsend.shape[1]
    lane_group = lax.broadcasted_iota(jnp.int32, (run, targets), 1) // tcols
    for panel in range(panels):
        packed = jnp.zeros((run, targets), F32)
        for g in range(n_pts):
            begin = (panel * n_pts + g) * run
            packed = packed + jnp.where(lane_group == g, window[begin:begin + run], 0.0)
        wsend[panel] = packed.astype(BF16)

    def w_copy(c_src, c_dst):
        return remote(
            wsend.at[c_dst // owners], wrecv.at[c_src], w_s.at[c_dst], w_r.at[c_src], p_me, c_dst
        )
    each(n_ctr - 1, lambda k: w_copy(c_me, peer(k)).start())
    wrecv[c_me] = wsend[my_panel]

    tall = lax.broadcasted_iota(jnp.int32, (tcols, targets), 1)
    first = lax.broadcasted_iota(jnp.int32, (tcols, targets), 0)
    pick_t = (tall == p_me * tcols + first).astype(BF16)
    wide_t = dot_nt(pick_t, rall[...]).astype(BF16)

    def backward(k):
        at = pl.ds(pl.multiple_of(k * chunk, chunk), chunk)
        grad_ref[:, at] = jnp.dot(wide_t, kmat[:, at], preferred_element_type=F32)
    each(chunks, backward)

    each(n_ctr - 1, lambda k: w_copy(peer(k), peer(k)).wait_recv())
    for o in range(n_ctr):
        wpack[pl.ds(o, run, stride=n_ctr), :] = wrecv[order_ref[o]].astype(F32)

    def so_copy(c_src, c_dst):
        return remote(solsend, solrecv.at[c_src], so_s.at[c_dst], so_r.at[c_src], p_me, c_dst)

    def rh_copy(c_src, c_dst):
        at = lax.rem(c_src, owners)
        return remote(rhssend, rhsrecv.at[at], rh_s.at[c_dst], rh_r.at[at], p_me, c_dst)

    for panel in range(panels):
        @pl.when(my_panel == panel)
        def _():
            if panel == 0:
                turned = wpack[...].T.astype(BF16)
                rhs = jnp.concatenate([turned[g * tcols:(g + 1) * tcols] for g in range(n_pts)], axis=1)
            else:
                local = (c_me - panel * owners) * own_rows
                part_len = panel_rows // n_pts
                within = pl.multiple_of(lax.rem(local, part_len), own_rows)
                turned = wpack[pl.ds(within, own_rows), :].T
                for g in range(n_pts):
                    wblk[g] = turned[g * tcols:(g + 1) * tcols]
                own = wblk[local // part_len]
                done = panel * owners
                each(done, lambda k: so_copy(k, k).wait_recv())
                solved = jnp.concatenate([solrecv[b] for b in range(done)], axis=1)
                own = own - dot_nt(solved, fac[:, :done * own_rows])
                rhssend[...] = own.astype(BF16)

                def fellow(k):
                    return panel * owners + lax.rem(c_me - panel * owners + k + 1, owners)
                each(owners - 1, lambda k: rh_copy(c_me, fellow(k)).start())
                rhsrecv[c_me - panel * owners] = rhssend[...]
                each(owners - 1, lambda k: rh_copy(fellow(k), fellow(k)).wait_recv())
                rhs = jnp.concatenate([rhsrecv[b] for b in range(owners)], axis=1)
            result = dot_nt(rhs, pinv[...])
            sol_ref[...] = result
            later = (panels - 1 - panel) * owners
            if later:
                solsend[...] = result.astype(BF16)

                def after(k):
                    return (panel + 1) * owners + lax.rem(k + c_me, later)
                each(later, lambda k: so_copy(c_me, after(k)).start())
                each(later, lambda k: so_copy(c_me, after(k)).wait_send())
            if panel > 0:
                each(owners - 1, lambda k: rh_copy(c_me, fellow(k)).wait_send())

    each(n_ctr - 1, lambda k: pt_copy(c_me, peer(k)).wait_send())
    each(n_pts - 1, lambda k: fw_copy(p_me, mate(k)).wait_send())
    each(n_ctr - 1, lambda k: pr_copy(c_me, peer(k)).wait_send())
    each(everyone - 1, lambda k: rs_copy(me, other(k)).wait_send())
    each(n_ctr - 1, lambda k: w_copy(c_me, peer(k)).wait_send())


def body(
    points, point_class, targets, class_weight, inv_scale, centers, coefficients, center_index, factor, panel_inverse
):
    n_pts, n_ctr = lax.axis_size("pts"), lax.axis_size("ctr")
    rows, feats = points.shape
    n_cen, n_tgt = coefficients.shape
    tcols = n_tgt // n_pts
    own_rows, panel_rows = panel_inverse.shape
    panels = factor.shape[1] // panel_rows
    owners = panel_rows // own_rows
    everyone = n_pts * n_ctr
    total = rows * everyone
    slots = center_index.shape[0] // n_ctr
    run = slots // panels // n_pts
    solved_cols = panel_rows * (panels - 1)
    mine = lax.axis_index("ctr")
    order = center_index[:n_ctr] // n_cen
    table = center_index.reshape(slots, n_ctr)
    local = jnp.sum(jnp.where((order == mine)[None, :], table - mine * n_cen, 0), axis=1)
    chosen = centers.at[local].get(mode="promise_in_bounds")
    vmem = pl.BlockSpec(memory_space=pltpu.VMEM)
    hbm = pl.BlockSpec(memory_space=pl.ANY)
    dma = pltpu.SemaphoreType.DMA
    grad, solved = pl.pallas_call(
        functools.partial(kernel, n_pts, n_ctr, panels, 512),
        out_shape=(
            jax.ShapeDtypeStruct((tcols, n_cen), F32),
            jax.ShapeDtypeStruct((tcols, own_rows), F32),
        ),
        in_specs=[pl.BlockSpec(memory_space=pltpu.SMEM)] + [vmem] * 6 + [hbm] * 4,
        out_specs=(vmem, vmem),
        scratch_shapes=[
            pltpu.VMEM((n_cen, feats), BF16),
            pltpu.VMEM((n_cen, n_tgt), BF16),
            pltpu.VMEM((own_rows, panel_rows), F32),
            pltpu.VMEM((own_rows, panel_rows), BF16),
            pltpu.VMEM((own_rows, solved_cols), F32),
            pltpu.VMEM((own_rows, solved_cols), BF16),
            pltpu.VMEM((8, n_cen), F32),
            pltpu.VMEM((total, feats), BF16),
            pltpu.VMEM((total, n_cen), BF16),
            pltpu.VMEM((slots, total), BF16),
            pltpu.VMEM((n_ctr, rows, n_tgt), F32),
            pltpu.VMEM((n_ctr, rows, n_tgt), F32),
            pltpu.VMEM((total, n_tgt), BF16),
            pltpu.VMEM((panels, run, n_tgt), BF16),
            pltpu.VMEM((n_ctr, run, n_tgt), BF16),
            pltpu.VMEM((run * n_ctr, n_tgt), F32),
            pltpu.VMEM((n_pts, tcols, own_rows), F32),
            pltpu.VMEM((tcols, own_rows), BF16),
            pltpu.VMEM((owners * (panels - 1), tcols, own_rows), BF16),
            pltpu.VMEM((tcols, own_rows), BF16),
            pltpu.VMEM((owners, tcols, own_rows), BF16),
            dma((4,)),
            dma((n_ctr,)), dma((n_ctr,)),
            dma((n_pts,)), dma((n_pts,)),
            dma((n_ctr,)), dma((n_ctr,)),
            dma((everyone,)), dma((everyone,)),
            dma((n_ctr,)), dma((n_ctr,)),
            dma((n_ctr,)), dma((n_ctr,)),
            dma((n_ctr,)), dma((owners,)),
        ],
        compiler_params=pltpu.CompilerParams(
            collective_id=0, has_side_effects=True, vmem_limit_bytes=67043328
        ),
        name="falkon",
    )(
        order, points, point_class[:, None], targets, class_weight[None, :], inv_scale[None, :],
        chosen, centers, coefficients, factor, panel_inverse,
    )
    return grad.T, solved.T


def solution(mesh):
    placed = (
        P(("pts", "ctr"), None),
        P(("pts", "ctr")),
        P(("pts", "ctr"), None),
        P(),
        P(),
        P("ctr", None),
        P("ctr", None),
        P(),
        P("ctr", None),
        P("ctr", None),
    )
    return jax.shard_map(
        body,
        mesh=mesh,
        in_specs=placed,
        out_specs=(P("ctr", "pts"), P("ctr", "pts")),
        check_vma=False,
    )
```

time: 315 us -> 61.7 us (0.20)
  the two profiles are of different devices: /device:TPU:0 before, /device:TPU:18 now
where the time goes in v1:
time: 61.7 us; the launch traced here: 61.3 us
  Pallas kernels  48.4 us (78%)
  local copies, waits for them, and re-layouts  10.2 us (17%)
  other arithmetic  2.08 us (3%)
  between operations  0.67 us (1%)
    pallas_call x1, Pallas kernels, body(): pl.pallas_call(functools.partial(kernel, n_pts, n_ctr, panels, 512), out_...  48.4 us
    gather x1, local copies, waits for them, and re-layouts, body(): chosen = centers.at[local].get(mode='promise_in_bounds')  5.38 us
    unnamed x2, local copies, waits for them, and re-layouts  3.34 us
    broadcast_in_dim x1, local copies, waits for them, and re-layouts, body(): point_class[:, None]  1.33 us

profile of v1, /device:TPU:18, one launch (start us, length us, event | category | flops | bytes accessed | tf_op | source)
XLA Modules:
  0.0 61.3 jit_solution(9222251639571900751)
XLA Ops:
  0.6 1.2 %broadcast_compare_fusion = (pred[8]{0:T(512)(128)(4,1)S(1)}, s32[8]{0:T(128)}) fusion(s32[]{:T(128)S(6)} %axis_index.12, s32[4096]{0:T(1024)} %param.17), kind=kLoop, calls=%fused_computation.9 | loop fusion | flops 128 | bytes 76 | tf_op jit(solution)/shard_map/eq | solution.py:281
  1.8 1.3 %copy.13.cls_ref = s32[16,1]{1,0:T(8,128)} copy(s32[16,1]{0,1:T(1,128)} %bitcast.13) | data formatting | bytes 128 | tf_op jit(solution)/shard_map/broadcast_in_dim | solution.py:330
  3.2 0.7 %broadcast_subtract_fusion = s32[4096]{0:T(1024)S(1)} fusion(s32[4096]{0:T(1024)} %param.17, s32[]{:T(128)S(6)} %mul.3), kind=kLoop, calls=%fused_computation.3 | loop fusion | flops 4096 | bytes 32772 | tf_op jit(solution)/shard_map/sub | solution.py:281
  3.9 0.2 sub.16
  4.0 0.1 select_reduce_fusion
  4.2 5.4 %gather_fusion = bf16[512,512]{1,0:T(8,128)(2,1)} fusion(bf16[4096,512]{1,0:T(8,128)(2,1)} %cen_hbm.1, s32[1024]{0:T(1024)S(1)} %pad_clamp_fusion), kind=kCustom, calls=%fused_computation | custom fusion | bytes 1050624 | tf_op jit(solution)/shard_map/gather | solution.py:282
  9.6 48.4 %falkon.1 = (f32[32,4096]{1,0:T(8,128)}, f32[32,512]{1,0:T(8,128)}) custom-call(s32[8]{0:T(128)} %get-tuple-element.7.order_ref, bf16[16,512]{1,0:T(8,128)(2,1)} %pts_ref.1, s32[16,1]{1,0:T(8,128)} %copy.13.cls_ref, f32[16,128]{1,0:T(8,128)} %tgt_ref.1, f32[1,8]{1,0:T(1,128)} %bitcast.12, f32[1,512]{1,0:T(1,128)} %bitcast.11, bf16[512,512]{1,0:T(8,128)(2,1)} %gather_fusion, ...), custom_call_target="tpu_custom_call" | custom-call | tf_op jit(solution)/shard_map/falkon/pallas_call | solution.py:286
  58.0 1.9 %copy.16 = f32[4096,32]{0,1:T(8,128)} copy(f32[4096,32]{0,1:T(8,128)} %bitcast.7) | data formatting | bytes 1048576
  59.8 1.5 %copy.17 = f32[512,32]{0,1:T(8,128)} copy(f32[512,32]{0,1:T(8,128)} %bitcast.8) | data formatting | bytes 131072
  (2 shorter events, 0.0 us)

commit v2 on v1

--- a/solution.py
+++ b/solution.py
@@ -19,10 +19,10 @@
 
 def kernel(
     n_pts, n_ctr, panels, chunk,
-    order_ref, pts_ref, cls_ref, tgt_ref, cw_ref, inv_ref, sel_ref, cen_hbm, coef_hbm, fac_hbm, pinv_hbm,
+    pts_ref, cls_ref, tgt_ref, cw_ref, inv_ref, idx_ref, idx_hbm, cen_hbm, coef_hbm, fac_hbm, pinv_hbm,
     grad_ref, sol_ref,
     cen, coef, pinv_raw, pinv, fac_raw, fac, rnorm, pall, kmat, ksel,
-    part, part_recv, rall, wsend, wrecv, wpack, wblk, solsend, solrecv, rhssend, rhsrecv,
+    head, sel, part, part_recv, rall, wsend, wrecv, wpack, wblk, solsend, solrecv, rhssend, rhsrecv,
     loc, pt_s, pt_r, fw_s, fw_r, pr_s, pr_r, rs_s, rs_r, w_s, w_r, so_s, so_r, rh_s, rh_r,
 ):
     p_me, c_me = lax.axis_index("pts"), lax.axis_index("ctr")
@@ -60,14 +60,14 @@
             barrier, inc=1,
             device_id={"pts": other // n_ctr, "ctr": lax.rem(other, n_ctr)}, device_id_type=MESH,
         )
-    each(everyone - 1, greet)
-
     cen_copy = pltpu.make_async_copy(cen_hbm, cen, loc.at[0])
     coef_copy = pltpu.make_async_copy(coef_hbm, coef, loc.at[1])
     pinv_copy = pltpu.make_async_copy(pinv_hbm, pinv_raw, loc.at[2])
     fac_copy = pltpu.make_async_copy(fac_hbm.at[:, pl.ds(0, fac.shape[1])], fac_raw, loc.at[3])
-    for copy in (cen_copy, coef_copy, pinv_copy, fac_copy):
-        copy.start()
+    head_copy = pltpu.make_async_copy(idx_hbm.at[pl.ds(0, head.shape[0])], head, loc.at[4])
+    cen_copy.start()
+    each(everyone - 1, greet)
+    coef_copy.start()
 
     inv = inv_ref[...]
     own_slot = pl.ds(pl.multiple_of(me * rows, rows), rows)
@@ -95,6 +95,9 @@
         rnorm[:, at] = 0.5 * (dot_nt(ones, high) + dot_nt(ones, low))
     each(chunks, scale)
     coef_copy.wait()
+    pinv_copy.start()
+    fac_copy.start()
+    head_copy.start()
 
     each(n_ctr - 1, lambda k: pt_copy(peer(k), peer(k)).wait_recv())
 
@@ -105,9 +108,12 @@
         at = group_at(p_src)
         return remote(pall.at[at], pall.at[at], fw_s.at[p_dst], fw_r.at[p_src], p_dst, c_me)
 
+    pair = p_me // 2 * 2
+
     def mate(k):
-        return lax.rem(p_me + k + 1, n_pts)
-    each(n_pts - 1, lambda k: fw_copy(p_me, mate(k)).start())
+        return 2 * pair + 1 - p_me if k == 0 else lax.rem(pair + k + 1, n_pts)
+    for k in range(n_pts - 1):
+        fw_copy(p_me, mate(k)).start()
 
     def half_norm(x):
         return 0.5 * jnp.sum(jnp.square(x.astype(F32)), axis=1, keepdims=True)
@@ -130,16 +136,41 @@
         return remote(part.at[c_dst], part_recv.at[c_src], pr_s.at[c_dst], pr_r.at[c_src], p_me, c_dst)
     each(n_ctr - 1, lambda k: pr_copy(c_me, peer(k)).start())
 
-    pinv_copy.wait()
-    pinv[...] = pinv_raw[...].astype(BF16)
-    fac_copy.wait()
-    fac[...] = fac_raw[...].astype(BF16)
+    shift, wide_lanes = 64, idx_ref.shape[1]
+    per = wide_lanes // n_ctr
+    slots = sel.shape[0]
+    relative = idx_ref[...] - c_me * centers
+    relative = jnp.where((relative >= 0) & (relative < centers), relative, 0)
+
+    def iota(shape, dim):
+        return lax.broadcasted_iota(jnp.int32, shape, dim)
+
+    def hot(mask):
+        return jnp.where(mask, 1.0, 0.0).astype(BF16)
+    fold = hot(iota((wide_lanes, wide_lanes), 0) // n_ctr == iota((wide_lanes, wide_lanes), 1))
+    spread = hot(iota((slots, relative.shape[0]), 0) // per == iota((slots, relative.shape[0]), 1))
+
+    def column(value):
+        folded = jnp.dot(value.astype(F32).astype(BF16), fold, preferred_element_type=F32)
+        return jnp.dot(spread, folded.astype(BF16), preferred_element_type=F32)
+    both = shift * column(relative // shift) + column(lax.rem(relative, shift))
+    at_lane = lax.rem(iota((slots, wide_lanes), 0), per) == iota((slots, wide_lanes), 1)
+    local_row = jnp.sum(jnp.where(at_lane, both, 0.0), axis=1, keepdims=True).astype(jnp.int32)
+    sel[...] = jnp.zeros_like(sel)
+
+    def select(k):
+        at = pl.ds(pl.multiple_of(k * chunk, chunk), chunk)
+        picked = hot(iota((slots, chunk), 1) == local_row - k * chunk)
+        sel[...] += jnp.dot(picked, cen[at, :], preferred_element_type=F32)
+    each(chunks, select)
 
     each(n_ctr - 1, lambda k: pr_copy(peer(k), peer(k)).wait_recv())
     part_recv[c_me] = part[c_me]
     predicted = jnp.sum(part_recv[...], axis=0)
+    same = iota((rows, rows), 0) == iota((rows, rows), 1)
+    own_class = jnp.sum(jnp.where(same, cls_ref[...], 0), axis=1, keepdims=True)
     classes = lax.broadcasted_iota(jnp.int32, (rows, cw_ref.shape[1]), 1)
-    weight = jnp.sum(jnp.where(cls_ref[...] == classes, cw_ref[...], 0.0), axis=1, keepdims=True)
+    weight = jnp.sum(jnp.where(own_class == classes, cw_ref[...], 0.0), axis=1, keepdims=True)
     rall[own_slot, :] = (weight * (predicted - tgt_ref[...])).astype(BF16)
 
     def rs_copy(src, dst):
@@ -152,13 +183,11 @@
         return lax.rem(me + k + 1, everyone)
     each(everyone - 1, lambda k: rs_copy(me, other(k)).start())
 
-    each(n_pts - 1, lambda k: fw_copy(mate(k), mate(k)).wait_recv())
-
-    def rest(k):
-        kernel_block(mate(k // chunks), lax.rem(k, chunks))
-    each((n_pts - 1) * chunks, rest)
-
-    chosen = (sel_ref[...].astype(F32) * inv).astype(BF16)
+    for k in range(n_pts - 1):
+        fw_copy(mate(k), mate(k)).wait_recv()
+        each(chunks, functools.partial(kernel_block, mate(k)))
+
+    chosen = sel[...].astype(BF16)
     chosen_norm = half_norm(chosen)
 
     def window_kernel(p):
@@ -202,10 +231,14 @@
         at = pl.ds(pl.multiple_of(k * chunk, chunk), chunk)
         grad_ref[:, at] = jnp.dot(wide_t, kmat[:, at], preferred_element_type=F32)
     each(chunks, backward)
+    pinv_copy.wait()
+    fac_copy.wait()
+    head_copy.wait()
+    pinv[...] = pinv_raw[...].astype(BF16)
 
     each(n_ctr - 1, lambda k: w_copy(peer(k), peer(k)).wait_recv())
     for o in range(n_ctr):
-        wpack[pl.ds(o, run, stride=n_ctr), :] = wrecv[order_ref[o]].astype(F32)
+        wpack[pl.ds(o, run, stride=n_ctr), :] = wrecv[head[o // wide_lanes, o % wide_lanes] // centers].astype(F32)
 
     def so_copy(c_src, c_dst):
         return remote(solsend, solrecv.at[c_src], so_s.at[c_dst], so_r.at[c_src], p_me, c_dst)
@@ -229,6 +262,7 @@
                     wblk[g] = turned[g * tcols:(g + 1) * tcols]
                 own = wblk[local // part_len]
                 done = panel * owners
+                fac[...] = fac_raw[...].astype(BF16)
                 each(done, lambda k: so_copy(k, k).wait_recv())
                 solved = jnp.concatenate([solrecv[b] for b in range(done)], axis=1)
                 own = own - dot_nt(solved, fac[:, :done * own_rows])
@@ -254,7 +288,8 @@
                 each(owners - 1, lambda k: rh_copy(c_me, fellow(k)).wait_send())
 
     each(n_ctr - 1, lambda k: pt_copy(c_me, peer(k)).wait_send())
-    each(n_pts - 1, lambda k: fw_copy(p_me, mate(k)).wait_send())
+    for k in range(n_pts - 1):
+        fw_copy(p_me, mate(k)).wait_send()
     each(n_ctr - 1, lambda k: pr_copy(c_me, peer(k)).wait_send())
     each(everyone - 1, lambda k: rs_copy(me, other(k)).wait_send())
     each(n_ctr - 1, lambda k: w_copy(c_me, peer(k)).wait_send())
@@ -275,60 +310,59 @@
     slots = center_index.shape[0] // n_ctr
     run = slots // panels // n_pts
     solved_cols = panel_rows * (panels - 1)
-    mine = lax.axis_index("ctr")
-    order = center_index[:n_ctr] // n_cen
-    table = center_index.reshape(slots, n_ctr)
-    local = jnp.sum(jnp.where((order == mine)[None, :], table - mine * n_cen, 0), axis=1)
-    chosen = centers.at[local].get(mode="promise_in_bounds")
+    index = center_index.reshape(-1, 128)
     vmem = pl.BlockSpec(memory_space=pltpu.VMEM)
     hbm = pl.BlockSpec(memory_space=pl.ANY)
     dma = pltpu.SemaphoreType.DMA
+    scratch = [
+        pltpu.VMEM((n_cen, feats), BF16),
+        pltpu.VMEM((n_cen, n_tgt), BF16),
+        pltpu.VMEM((own_rows, panel_rows), F32),
+        pltpu.VMEM((own_rows, panel_rows), BF16),
+        pltpu.VMEM((own_rows, solved_cols), F32),
+        pltpu.VMEM((own_rows, solved_cols), BF16),
+        pltpu.VMEM((8, n_cen), F32),
+        pltpu.VMEM((total, feats), BF16),
+        pltpu.VMEM((total, n_cen), BF16),
+        pltpu.VMEM((slots, total), BF16),
+        pltpu.SMEM((8, 128), jnp.int32),
+        pltpu.VMEM((slots, feats), F32),
+        pltpu.VMEM((n_ctr, rows, n_tgt), F32),
+        pltpu.VMEM((n_ctr, rows, n_tgt), F32),
+        pltpu.VMEM((total, n_tgt), BF16),
+        pltpu.VMEM((panels, run, n_tgt), BF16),
+        pltpu.VMEM((n_ctr, run, n_tgt), BF16),
+        pltpu.VMEM((run * n_ctr, n_tgt), F32),
+        pltpu.VMEM((n_pts, tcols, own_rows), F32),
+        pltpu.VMEM((tcols, own_rows), BF16),
+        pltpu.VMEM((owners * (panels - 1), tcols, own_rows), BF16),
+        pltpu.VMEM((tcols, own_rows), BF16),
+        pltpu.VMEM((owners, tcols, own_rows), BF16),
+        dma((5,)),
+        dma((n_ctr,)), dma((n_ctr,)),
+        dma((n_pts,)), dma((n_pts,)),
+        dma((n_ctr,)), dma((n_ctr,)),
+        dma((everyone,)), dma((everyone,)),
+        dma((n_ctr,)), dma((n_ctr,)),
+        dma((n_ctr,)), dma((n_ctr,)),
+        dma((n_ctr,)), dma((owners,)),
+    ]
     grad, solved = pl.pallas_call(
         functools.partial(kernel, n_pts, n_ctr, panels, 512),
         out_shape=(
             jax.ShapeDtypeStruct((tcols, n_cen), F32),
             jax.ShapeDtypeStruct((tcols, own_rows), F32),
         ),
-        in_specs=[pl.BlockSpec(memory_space=pltpu.SMEM)] + [vmem] * 6 + [hbm] * 4,
+        in_specs=[vmem] * 6 + [hbm] * 5,
         out_specs=(vmem, vmem),
-        scratch_shapes=[
-            pltpu.VMEM((n_cen, feats), BF16),
-            pltpu.VMEM((n_cen, n_tgt), BF16),
-            pltpu.VMEM((own_rows, panel_rows), F32),
-            pltpu.VMEM((own_rows, panel_rows), BF16),
-            pltpu.VMEM((own_rows, solved_cols), F32),
-            pltpu.VMEM((own_rows, solved_cols), BF16),
-            pltpu.VMEM((8, n_cen), F32),
-            pltpu.VMEM((total, feats), BF16),
-            pltpu.VMEM((total, n_cen), BF16),
-            pltpu.VMEM((slots, total), BF16),
-            pltpu.VMEM((n_ctr, rows, n_tgt), F32),
-            pltpu.VMEM((n_ctr, rows, n_tgt), F32),
-            pltpu.VMEM((total, n_tgt), BF16),
-            pltpu.VMEM((panels, run, n_tgt), BF16),
-            pltpu.VMEM((n_ctr, run, n_tgt), BF16),
-            pltpu.VMEM((run * n_ctr, n_tgt), F32),
-            pltpu.VMEM((n_pts, tcols, own_rows), F32),
-            pltpu.VMEM((tcols, own_rows), BF16),
-            pltpu.VMEM((owners * (panels - 1), tcols, own_rows), BF16),
-            pltpu.VMEM((tcols, own_rows), BF16),
-            pltpu.VMEM((owners, tcols, own_rows), BF16),
-            dma((4,)),
-            dma((n_ctr,)), dma((n_ctr,)),
-            dma((n_pts,)), dma((n_pts,)),
-            dma((n_ctr,)), dma((n_ctr,)),
-            dma((everyone,)), dma((everyone,)),
-            dma((n_ctr,)), dma((n_ctr,)),
-            dma((n_ctr,)), dma((n_ctr,)),
-            dma((n_ctr,)), dma((owners,)),
-        ],
+        scratch_shapes=scratch,
         compiler_params=pltpu.CompilerParams(
             collective_id=0, has_side_effects=True, vmem_limit_bytes=67043328
         ),
         name="falkon",
     )(
-        order, points, point_class[:, None], targets, class_weight[None, :], inv_scale[None, :],
-        chosen, centers, coefficients, factor, panel_inverse,
+        points, point_class[None, :], targets, class_weight[None, :], inv_scale[None, :],
+        index, index, centers, coefficients, factor, panel_inverse,
     )
     return grad.T, solved.T
 

time: 61.7 us -> 52.5 us (0.85)
  local copies, waits for them, and re-layouts: 10.2 us -> 3.34 us
  other arithmetic: 2.08 us -> 0 us
    gather x1 -> x0, local copies, waits for them, and re-layouts: 5.38 us -> none  [body(): chosen = centers.at[local].get(mode='promise_in_bounds')]
    broadcast_in_dim x1 -> x0, local copies, waits for them, and re-layouts: 1.33 us -> none  [body(): point_class[:, None]]
    eq x1 -> x0, other arithmetic: 1.2 us -> none  [body(): order == mine]
    sub x1 -> x0, other arithmetic: 0.72 us -> none  [body(): table - mine * n_cen]
where the time goes in v2:
time: 52.5 us; the launch traced here: 52.2 us
  Pallas kernels  48.2 us (92%)
  local copies, waits for them, and re-layouts  3.34 us (6%)
  between operations  0.64 us (1%)
    pallas_call x1, Pallas kernels, body(): pl.pallas_call(functools.partial(kernel, n_pts, n_ctr, panels, 512), out_...  48.2 us
    unnamed x2, local copies, waits for them, and re-layouts  3.34 us

profile of v2, /device:TPU:18, one launch (start us, length us, event | category | flops | bytes accessed | tf_op | source)
XLA Modules:
  0.0 52.2 jit_solution(6607124335557245995)
XLA Ops:
  0.6 48.2 %falkon.1 = (f32[32,4096]{1,0:T(8,128)}, f32[32,512]{1,0:T(8,128)}) custom-call(bf16[16,512]{1,0:T(8,128)(2,1)} %pts_ref.1, s32[1,16]{1,0:T(1,128)} %bitcast.11, f32[16,128]{1,0:T(8,128)} %tgt_ref.1, f32[1,8]{1,0:T(1,128)} %bitcast.12, f32[1,512]{1,0:T(1,128)} %bitcast.10, s32[32,128]{1,0:T(8,128)} %bitcast.7, s32[32,128]{1,0:T(8,128)} %bitcast.8, ...), custom_call_target="tpu_custom_call" | custom-call | tf_op jit(solution)/shard_map/falkon/pallas_call | solution.py:350
  48.8 1.9 %copy.14 = f32[4096,32]{0,1:T(8,128)} copy(f32[4096,32]{0,1:T(8,128)} %bitcast.6) | data formatting | bytes 1048576
  50.7 1.5 %copy.15 = f32[512,32]{0,1:T(8,128)} copy(f32[512,32]{0,1:T(8,128)} %bitcast.9) | data formatting | bytes 131072

commit v3 on v2

--- a/solution.py
+++ b/solution.py
@@ -348,7 +348,7 @@
         dma((n_ctr,)), dma((owners,)),
     ]
     grad, solved = pl.pallas_call(
-        functools.partial(kernel, n_pts, n_ctr, panels, 512),
+        functools.partial(kernel, n_pts, n_ctr, panels, 1024),
         out_shape=(
             jax.ShapeDtypeStruct((tcols, n_cen), F32),
             jax.ShapeDtypeStruct((tcols, own_rows), F32),

time: 52.5 us -> 49.1 us (0.935)
  Pallas kernels: 48.2 us -> 44.8 us
    pallas_call x1, Pallas kernels: 48.2 us -> 44.8 us  [body(): pl.pallas_call(functools.partial(kernel, n_pts, n_ctr, panels, 1024), out...]
where the time goes in v3:
time: 49.1 us; the launch traced here: 48.8 us
  Pallas kernels  44.8 us (91%)
  local copies, waits for them, and re-layouts  3.34 us (7%)
  between operations  0.64 us (1%)
    pallas_call x1, Pallas kernels, body(): pl.pallas_call(functools.partial(kernel, n_pts, n_ctr, panels, 1024), out...  44.8 us
    unnamed x2, local copies, waits for them, and re-layouts  3.34 us

profile of v3, /device:TPU:18, one launch (start us, length us, event | category | flops | bytes accessed | tf_op | source)
XLA Modules:
  0.0 48.8 jit_solution(11285277159207758075)
XLA Ops:
  0.6 44.8 %falkon.1 = (f32[32,4096]{1,0:T(8,128)}, f32[32,512]{1,0:T(8,128)}) custom-call(bf16[16,512]{1,0:T(8,128)(2,1)} %pts_ref.1, s32[1,16]{1,0:T(1,128)} %bitcast.11, f32[16,128]{1,0:T(8,128)} %tgt_ref.1, f32[1,8]{1,0:T(1,128)} %bitcast.12, f32[1,512]{1,0:T(1,128)} %bitcast.10, s32[32,128]{1,0:T(8,128)} %bitcast.7, s32[32,128]{1,0:T(8,128)} %bitcast.8, ...), custom_call_target="tpu_custom_call" | custom-call | tf_op jit(solution)/shard_map/falkon/pallas_call | solution.py:350
  45.5 1.9 %copy.14 = f32[4096,32]{0,1:T(8,128)} copy(f32[4096,32]{0,1:T(8,128)} %bitcast.6) | data formatting | bytes 1048576
  47.3 1.5 %copy.15 = f32[512,32]{0,1:T(8,128)} copy(f32[512,32]{0,1:T(8,128)} %bitcast.9) | data formatting | bytes 131072
